TPU v7x, 32 devices: a whole 2x2x4 slice. The times are simulated.
32 devices in a mesh: dp: 4 (over z), table: 8 (over y, x, core).
Axes of the slice: x: 2, y: 2, z: 4, core: 2. Of those that a mesh axis runs over, the one named last changes fastest.
Arguments:
- item_emb: bfloat16 [16384, 512], P(('dp', 'table')), may hold values from -6 to 6
- cotangent: bfloat16 [16384, 512], P(('dp', 'table')), may hold values from -6 to 6
- in_proj: bfloat16 [512, 2048], replicated, may hold values from -0.25 to 0.25
- out_proj: bfloat16 [512, 512], replicated, may hold values from -0.25 to 0.25
- history_lengths: int32 [32, 8], P(('dp', 'table')), may hold values from 1 to 256, 512 in all within a row
- item_ids: int32 [16384], P(('dp', 'table')), may hold values from 0 to 32767, as said below
Outputs:
- emb_grad: float32 [32768, 512], P(('dp', 'table'))
- in_grad: float32 [512, 2048], replicated
- out_grad: float32 [512, 512], replicated
Inputs may be any that keep to these rules, and one draw needn't show every extreme that they name: `item_ids`: among the 512 items of one device, at most 32 have ids of one device's rows (ids r with the same r // 1024), and these name at most 16 distinct ids; in every draw some device's rows get exactly 32 items with 16 distinct ids from every device. `history_lengths`: each row sums to 512.
All inputs are finite; a program needn't handle non-finite values.
Results may differ from a plain program's by a relative error of at most 0.0075.
Values sent between devices are 32-bit elements; how exact they have to be, the bound alone decides.
No kernel may reach another device: no remote copies, remote signals or barrier semaphores. Data moves between devices by JAX's collectives and lax.ppermute only.
A program may use at most 64 MiB of HBM per device.

v0:
```python
import math
import jax
import jax.numpy as jnp
from jax import lax
from jax.sharding import PartitionSpec as P

H = 4
OWN_ROWS = 1024
BLOCK = 512
LEN = 256
norm_eps = 1e-05


def silu_grad(pre_value):
    sigmoid_z = jax.nn.sigmoid(pre_value)
    return sigmoid_z * (1.0 + pre_value * (1.0 - sigmoid_z))


def block_grads(hidden, pre_act, cot_rows, lengths, out_proj):
    block_rows = hidden.shape[0]
    model_width = cot_rows.shape[1]
    head_size = model_width // H
    gating = hidden[:, :model_width].astype(jnp.float32)
    value_vecs = hidden[:, model_width : 2 * model_width].reshape(block_rows, H, head_size)
    query_vecs = hidden[:, 2 * model_width : 3 * model_width].reshape(block_rows, H, head_size)
    key_vecs = hidden[:, 3 * model_width :].reshape(block_rows, H, head_size)
    positions = jnp.arange(block_rows, dtype=jnp.int32)
    seq_ends = jnp.cumsum(lengths)
    segment = jnp.sum((positions[:, None] >= seq_ends[None, :]).astype(jnp.int32), axis=1)
    causal_mask = (
        (segment[:, None] == segment[None, :]) & (positions[None, :] <= positions[:, None])
    ).astype(jnp.float32) * (1.0 / LEN)
    score_scale = 1.0 / math.sqrt(head_size)
    scores = (
        jnp.einsum("ihd,jhd->hij", query_vecs, key_vecs, preferred_element_type=jnp.float32)
        * score_scale
    )
    weights = (jax.nn.silu(scores) * causal_mask).astype(jnp.bfloat16)
    attended = jnp.einsum(
        "hij,jhd->ihd", weights, value_vecs, preferred_element_type=jnp.float32
    ).reshape(block_rows, model_width)
    row_mean = jnp.mean(attended, axis=1, keepdims=True)
    centered = attended - row_mean
    inv_std = lax.rsqrt(jnp.mean(centered * centered, axis=1, keepdims=True) + norm_eps)
    normed = centered * inv_std
    gated_out = (normed * gating).astype(jnp.bfloat16)
    grad_out = lax.dot_general(
        cot_rows, out_proj, (((1,), (1,)), ((), ())), preferred_element_type=jnp.float32
    )
    grad_gate = grad_out * normed
    grad_norm = grad_out * gating
    grad_att = inv_std * (
        grad_norm
        - jnp.mean(grad_norm, axis=1, keepdims=True)
        - normed * jnp.mean(grad_norm * normed, axis=1, keepdims=True)
    )
    grad_att = grad_att.astype(jnp.bfloat16).reshape(block_rows, H, head_size)
    grad_weights = jnp.einsum(
        "ihd,jhd->hij", grad_att, value_vecs, preferred_element_type=jnp.float32
    )
    grad_value = jnp.einsum("hij,ihd->jhd", weights, grad_att, preferred_element_type=jnp.float32)
    grad_scores = (grad_weights * causal_mask * silu_grad(scores)).astype(jnp.bfloat16)
    grad_query = (
        jnp.einsum("hij,jhd->ihd", grad_scores, key_vecs, preferred_element_type=jnp.float32)
        * score_scale
    )
    grad_key = (
        jnp.einsum("hij,ihd->jhd", grad_scores, query_vecs, preferred_element_type=jnp.float32)
        * score_scale
    )
    grad_hidden = jnp.concatenate(
        [
            grad_gate,
            grad_value.reshape(block_rows, model_width),
            grad_query.reshape(block_rows, model_width),
            grad_key.reshape(block_rows, model_width),
        ],
        axis=1,
    )
    grad_pre = (grad_hidden * silu_grad(pre_act)).astype(jnp.bfloat16)
    return (gated_out, grad_pre)


def place_rows(row_values, owner_of, local_row, owners, capacity):
    model_width = row_values.shape[1]
    onehot = (owner_of[:, None] == jnp.arange(owners, dtype=jnp.int32)[None, :]).astype(jnp.int32)
    before = jnp.cumsum(onehot, axis=0) - onehot
    slot_rank = jnp.sum(before * onehot, axis=1)
    slot_index = jnp.where(owner_of < owners, owner_of * capacity + slot_rank, owners * capacity)
    slot_rows = (
        jnp.zeros((owners * capacity, model_width), jnp.float32)
        .at[slot_index]
        .set(row_values, mode="drop")
    )
    slot_ids = (
        jnp.full((owners * capacity,), OWN_ROWS, jnp.int32)
        .at[slot_index]
        .set(local_row, mode="drop")
    )
    return (slot_rows.reshape(owners, capacity, model_width), slot_ids.reshape(owners, capacity))


def per_device(item_emb, cotangent, in_proj, out_proj, history_lengths, item_ids):
    rows_here = item_emb.shape[0]
    model_width = item_emb.shape[1]
    block_count = rows_here // BLOCK
    dp_count = lax.axis_size("dp")
    table_count = lax.axis_size("table")
    owners = dp_count * table_count
    capacity = 2 * rows_here // owners
    pre_act = jnp.dot(item_emb, in_proj, preferred_element_type=jnp.float32)
    hidden = jax.nn.silu(pre_act).astype(jnp.bfloat16)

    def one_block(pieces):
        return block_grads(pieces[0], pieces[1], pieces[2], pieces[3], out_proj)

    gated_out, grad_pre = lax.map(
        one_block,
        (
            hidden.reshape(block_count, BLOCK, 4 * model_width),
            pre_act.reshape(block_count, BLOCK, 4 * model_width),
            cotangent.reshape(block_count, BLOCK, model_width),
            history_lengths,
        ),
    )
    gated_out = gated_out.reshape(rows_here, model_width)
    grad_pre = grad_pre.reshape(rows_here, 4 * model_width)
    out_local = lax.dot_general(
        gated_out, cotangent, (((0,), (0,)), ((), ())), preferred_element_type=jnp.float32
    )
    in_local = lax.dot_general(
        item_emb, grad_pre, (((0,), (0,)), ((), ())), preferred_element_type=jnp.float32
    )
    in_total, out_total = lax.psum((in_local, out_local), ("dp", "table"))
    item_grad = lax.dot_general(
        grad_pre, in_proj, (((1,), (1,)), ((), ())), preferred_element_type=jnp.float32
    ) + cotangent.astype(jnp.float32)
    send_rows, send_ids = place_rows(
        item_grad, item_ids // OWN_ROWS, item_ids % OWN_ROWS, owners, capacity
    )
    arrived_rows, arrived_ids = (
        lax.all_to_all(send_rows, ("dp", "table"), split_axis=0, concat_axis=0, tiled=True),
        lax.all_to_all(send_ids, ("dp", "table"), split_axis=0, concat_axis=0, tiled=True),
    )
    emb_grad = (
        jnp.zeros((OWN_ROWS, model_width), jnp.float32)
        .at[arrived_ids.reshape(-1)]
        .add(arrived_rows.reshape(-1, model_width), mode="drop")
    )
    grad_scale = 1.0 / math.sqrt(rows_here * owners)
    return (emb_grad, in_total * grad_scale, out_total * grad_scale)


def solution(mesh):
    placed = (
        P(("dp", "table"), None),
        P(("dp", "table"), None),
        P(),
        P(),
        P(("dp", "table"), None),
        P(("dp", "table")),
    )
    return jax.shard_map(
        per_device,
        mesh=mesh,
        in_specs=placed,
        out_specs=(P(("dp", "table"), None), P(), P()),
        check_vma=False,
    )
```

profile of v0, /device:TPU:0, one launch (start us, length us, event | category | flops | bytes accessed | tf_op | source)
XLA Modules:
  0.0 264.7 jit_solution(13353558803683191540)
XLA Ops:
  7.2 0.0 copy-start
  7.2 0.8 add_select_fusion
  8.0 1.2 reduce-window.18
  9.2 0.2 slice_reduce_fusion
  9.5 0.1 fusion.15
  9.6 2.4 scatter_custom_fusion
  12.0 0.7 all_to_all.9
  12.7 7.3 %all-to-all-start = ((s32[32,1,32]{2,1,0:T(1,128)}), s32[32,1,32]{2,1,0:T(1,128)S(1)}, u32[]{:S(2)}, u32[]{:S(2)}) async-start(s32[32,1,32]{2,1,0:T(1,128)} %all_to_all.9), calls=%async_computation | async-start | bytes 32768 | tf_op jit(solution)/shard_map/all_to_all | solution.py:143
  20.0 0.0 copy-done
  20.0 0.0 copy-start.13
  20.0 4.9 %multiply_convert_fusion.2 = (bf16[512,2048]{0,1:T(8,128)(2,1)S(1)}, f32[512,2048]{0,1:T(8,128)}) fusion(bf16[512,512]{1,0:T(8,128)(2,1)} %param.6, bf16[512,2048]{1,0:T(8,128)(2,1)S(1)} %copy-done), kind=kOutput, calls=%fused_computation.8 | convolution fusion | flops 1078984704 | bytes 8912896 | tf_op jit(solution)/shard_map/dot_general | solution.py:111
  24.9 0.0 copy-start.3
  24.9 1.3 copy-done.3
  26.3 0.9 fusion.20
  27.2 0.0 copy-start.6
  27.2 0.0 copy-done.13
  27.2 0.2 reduce-window.20
  27.3 0.1 convert_reduce_fusion
  27.4 0.2 fusion.10
  27.6 0.3 copy-done.6
  27.9 1.6 multiply_convert_fusion.1
  29.5 0.0 copy-done.8
  29.5 0.0 copy-start.4
  29.6 0.0 copy-start.5
  29.6 0.0 copy-start.12
  29.6 0.0 copy-done.10
  29.6 0.8 fusion.21
  30.4 0.2 fusion.4
  30.6 0.5 copy-done.4
  31.1 0.1 copy-done.5
  31.2 0.2 copy-done.12
  31.4 0.6 fusion.12
  32.0 0.3 multiply_convert_fusion.3
  32.4 0.4 fusion.22
  32.8 0.0 copy-start.9
  32.8 0.0 copy-start.7
  32.8 1.9 multiply_convert_fusion
  34.7 0.0 copy-done.9
  34.7 0.0 copy-start.2
  34.7 0.8 convolution_multiply_fusion.1
  35.5 0.0 copy-done.7
  35.6 0.4 convolution_multiply_fusion
  36.0 0.9 copy-done.2
  36.9 1.5 fusion
  38.4 0.0 copy-start.1
  38.5 1.3 copy-done.1
  39.8 2.3 convolution_add_fusion
  42.1 4.5 %scatter_custom_fusion.1 = f32[1024,512]{1,0:T(8,128)} fusion(s32[512]{0:T(512)S(1)} %compare_select_fusion.1, f32[512,512]{1,0:T(8,128)} %convolution_add_fusion, f32[]{:T(128)} %constant.80.clone.1), kind=kCustom, calls=%fused_computation.28 | custom fusion | bytes 2097664 | tf_op jit(solution)/shard_map/scatter | solution.py:93
  46.6 0.0 all-to-all-done
  46.6 6.0 %all-to-all-start.1 = ((f32[32,32,512]{2,1,0:T(8,128)}), f32[32,32,512]{2,1,0:T(8,128)}, u32[]{:S(2)}, u32[]{:S(2)}) async-start(f32[32,32,512]{2,1,0:T(8,128)} %bitcast.81), calls=%async_computation.1 | async-start | bytes 4194304 | tf_op jit(solution)/shard_map/all_to_all | solution.py:142
  52.5 0.0 all-reduce.3.cloned.1.call-start
  52.6 1.4 fusion.23
  54.0 4.9 %convolution_bitcast_fusion = f32[512,2048]{0,1:T(8,128)} fusion(bf16[512,2048]{0,1:T(8,128)(2,1)} %copy-done.1, bf16[512,512]{1,0:T(8,128)(2,1)} %param.6), kind=kOutput, calls=%fused_computation.10 | convolution fusion | flops 1073741824 | bytes 6815744 | tf_op jit(solution)/shard_map/dot_general | solution.py:131
  58.9 0.0 all-reduce.3.cloned.1.call-update
  59.0 0.5 broadcast.203
  59.5 0.7 reduce.8
  60.1 0.1 reshape.200
  60.2 177.8 %all-reduce.3.cloned.1.call-done = (f32[512,2048]{0,1:T(8,128)}, f32[512,512]{1,0:T(8,128)}) async-done(((f32[512,2048]{0,1:T(8,128)}, f32[512,512]{1,0:T(8,128)}), (f32[512,2048]{0,1:T(8,128)}, f32[512,512]{1,0:T(8,128)})) %all-reduce.3.cloned.1.call-update) | async-done | bytes 5242896 | tf_op jit(solution)/shard_map/psum | solution.py:134
  238.1 4.7 %broadcast_multiply_fusion = f32[512,2048]{0,1:T(8,128)} fusion(f32[512,2048]{0,1:T(8,128)} %get-tuple-element.38), kind=kLoop, calls=%fused_computation.11 | loop fusion | flops 1048576 | bytes 8388608 | tf_op jit(solution)/shard_map/mul | solution.py:151
  242.7 5.4 %copy.34 = f32[512,2048]{1,0:T(8,128)} copy(f32[512,2048]{0,1:T(8,128)} %broadcast_multiply_fusion) | data formatting | bytes 8388608
  248.2 0.0 copy-done.11
  248.2 1.1 broadcast_multiply_fusion.1
  249.2 0.0 all-to-all-done.1
  249.2 8.7 %scatter_custom_fusion.2 = f32[1024,512]{1,0:T(8,128)} fusion(s32[1024]{0:T(1024)S(1)} %bitcast.94, f32[1024,512]{1,0:T(8,128)} %bitcast.18, f32[]{:T(128)} %constant.80.clone.1), kind=kCustom, calls=%fused_computation.26 | custom fusion | flops 524288 | bytes 2097664 | tf_op jit(solution)/shard_map/scatter-add | solution.py:148
  (11 shorter events, 0.1 us)
Async XLA Ops:
  7.2 12.9 %copy-start = (bf16[512,2048]{1,0:T(8,128)(2,1)S(1)}, bf16[512,2048]{1,0:T(8,128)(2,1)}, u32[]{:S(2)}) copy-start(bf16[512,2048]{1,0:T(8,128)(2,1)} %param.8) | copy-start | bytes 6291460
  12.7 33.8 %all-to-all-start = ((s32[32,1,32]{2,1,0:T(1,128)}), s32[32,1,32]{2,1,0:T(1,128)S(1)}, u32[]{:S(2)}, u32[]{:S(2)}) async-start(s32[32,1,32]{2,1,0:T(1,128)} %all_to_all.9), calls=%async_computation | async-start | bytes 32768 | tf_op jit(solution)/shard_map/all_to_all | solution.py:143
  20.0 7.1 %copy-start.13 = (s32[1,8]{1,0:T(1,128)S(1)}, s32[1,8]{1,0:T(1,128)}, u32[]{:S(2)}) copy-start(s32[1,8]{1,0:T(1,128)} %param.10) | copy-start | bytes 100
  24.9 1.3 copy-start.3
  27.2 0.8 copy-start.6
  27.2 2.4 copy-start.8
  27.9 1.6 copy-start.10
  29.5 1.6 copy-start.4
  29.6 1.7 copy-start.5
  29.6 1.8 copy-start.12
  32.8 1.9 copy-start.9
  32.8 2.7 %copy-start.7 = (bf16[512,512]{0,1:T(8,128)(2,1)S(1)}, bf16[512,512]{0,1:T(8,128)(2,1)}, u32[]{:S(2)}) copy-start(bf16[512,512]{0,1:T(8,128)(2,1)} %copy-done.6) | copy-start | bytes 1572868
  34.7 2.2 copy-start.2
  38.4 1.4 copy-start.1
  46.6 202.7 %all-to-all-start.1 = ((f32[32,32,512]{2,1,0:T(8,128)}), f32[32,32,512]{2,1,0:T(8,128)}, u32[]{:S(2)}, u32[]{:S(2)}) async-start(f32[32,32,512]{2,1,0:T(8,128)} %bitcast.81), calls=%async_computation.1 | async-start | bytes 4194304 | tf_op jit(solution)/shard_map/all_to_all | solution.py:142
  52.5 185.5 %all-reduce.3.cloned.1.call-start = ((), (), s32[]{:S(2)}) async-start(), calls=%async_computation.2 | async-start | bytes 10485760 | tf_op jit(solution)/shard_map/psum | solution.py:134
  242.7 5.4 %copy-start.11 = (f32[512,512]{1,0:T(8,128)S(1)}, f32[512,512]{1,0:T(8,128)}, u32[]{:S(2)}) copy-start(f32[512,512]{1,0:T(8,128)} %get-tuple-element.39) | copy-start | bytes 3145732
Sparse Core Ops, SparseCore 0:
  59.5 178.5 all-reduce.2
where the time goes:
time: 265 us
  waiting for transfers between devices  178 us (67%)
  matrix products  20.1 us (8%)
  other arithmetic  19.7 us (7%)
  local copies, waits for them, and re-layouts  19.5 us (7%)
  between operations  14.3 us (5%)
  starting transfers between devices  13.3 us (5%)
    psum x1, waiting for transfers between devices, per_device(): in_total, out_total = lax.psum((in_local, out_local), ('dp', 'table'))  178 us
    unnamed x29, local copies, waits for them, and re-layouts  10.1 us
    scatter-add x1, other arithmetic, per_device(): emb_grad = jnp.zeros((OWN_ROWS, model_width), jnp.float32).at[arrived_ids...  8.65 us
    all_to_all x1, starting transfers between devices, per_device(): lax.all_to_all(send_ids, ('dp', 'table'), split_axis=0, concat_axis=0, ti...  7.3 us
    all_to_all x1, starting transfers between devices, per_device(): lax.all_to_all(send_rows, ('dp', 'table'), split_axis=0, concat_axis=0, t...  5.96 us
    mul x2, other arithmetic, per_device(): return (emb_grad, in_total * grad_scale, out_total * grad_scale)  5.72 us
  transfers between devices with their start and end apart: 3, of which 1 were waited for; matrix products, arithmetic and copies ran while one was open for 15% of the time, Pallas kernels for 0%

commit v1 on v0

--- a/solution.py
+++ b/solution.py
@@ -3,12 +3,18 @@
 import jax.numpy as jnp
 from jax import lax
 from jax.sharding import PartitionSpec as P
+from jax.lax import psum
 
 H = 4
 OWN_ROWS = 1024
 BLOCK = 512
 LEN = 256
 norm_eps = 1e-05
+
+
+def extend_the_keys(x0):
+    response = psum(x0, axis_name="table")
+    return psum(response, axis_name="dp")
 
 
 def silu_grad(pre_value):
@@ -131,7 +137,7 @@
     in_local = lax.dot_general(
         item_emb, grad_pre, (((0,), (0,)), ((), ())), preferred_element_type=jnp.float32
     )
-    in_total, out_total = lax.psum((in_local, out_local), ("dp", "table"))
+    in_total, out_total = extend_the_keys((in_local, out_local))
     item_grad = lax.dot_general(
         grad_pre, in_proj, (((1,), (1,)), ((), ())), preferred_element_type=jnp.float32
     ) + cotangent.astype(jnp.float32)

time: 265 us -> 383 us (1.45)
  waiting for transfers between devices: 178 us -> 299 us
    all_to_all x1, waiting for transfers between devices: 0.01 us -> 104 us  [per_device(): lax.all_to_all(send_rows, ('dp', 'table'), split_axis=0, concat_axis=0, t...]
    psum x1 -> x2, waiting for transfers between devices: 178 us -> 195 us  [the longest x1 98.9 us: extend_the_keys(): return psum(response, axis_name='dp')]
  transfers between devices with their start and end apart: 3 -> 4, of which waited for: 1 -> 3; matrix products, arithmetic and copies ran while one was open for 15% -> 6% of each run, Pallas kernels for 0% -> 0%
where the time goes in v1:
time: 383 us; the launch traced here: 382 us
  waiting for transfers between devices  299 us (78%)
  matrix products  20 us (5%)
  local copies, waits for them, and re-layouts  19.5 us (5%)
  other arithmetic  18.9 us (5%)
  between operations  14.3 us (4%)
  starting transfers between devices  10.7 us (3%)
    all_to_all x1, waiting for transfers between devices, per_device(): lax.all_to_all(send_rows, ('dp', 'table'), split_axis=0, concat_axis=0, t...  104 us
    psum x1, waiting for transfers between devices, extend_the_keys(): return psum(response, axis_name='dp')  98.9 us
    psum x1, waiting for transfers between devices, extend_the_keys(): response = psum(x0, axis_name='table')  95.6 us
    unnamed x29, local copies, waits for them, and re-layouts  10.3 us
    scatter-add x1, other arithmetic, per_device(): emb_grad = jnp.zeros((OWN_ROWS, model_width), jnp.float32).at[arrived_ids...  8.65 us
  transfers between devices with their start and end apart: 4, of which 3 were waited for; matrix products, arithmetic and copies ran while one was open for 6% of the time, Pallas kernels for 0%

profile of v1, /device:TPU:0, one launch (start us, length us, event | category | flops | bytes accessed | tf_op | source)
XLA Modules:
  0.0 382.2 jit_solution(9665970615335697168)
XLA Ops:
  7.2 0.0 copy-start
  7.2 0.0 copy-start.13
  7.2 0.0 all-reduce.5.cloned.1.call-start
  7.2 1.5 copy-done
  8.8 4.9 %multiply_convert_fusion.2 = (bf16[512,2048]{0,1:T(8,128)(2,1)S(1)}, f32[512,2048]{0,1:T(8,128)}) fusion(bf16[512,512]{1,0:T(8,128)(2,1)} %param.6, bf16[512,2048]{1,0:T(8,128)(2,1)S(1)} %copy-done), kind=kOutput, calls=%fused_computation.8 | convolution fusion | flops 1078984704 | bytes 8912896 | tf_op jit(solution)/shard_map/dot_general | solution.py:117
  13.6 0.0 copy-start.3
  13.7 1.3 copy-done.3
  15.0 0.9 fusion.20
  15.9 0.0 copy-done.13
  15.9 0.2 reduce-window.20
  16.0 0.1 convert_reduce_fusion
  16.1 0.2 fusion.10
  16.3 0.3 copy-done.6
  16.7 1.6 multiply_convert_fusion.1
  18.2 0.0 copy-start.4
  18.3 0.0 copy-start.5
  18.3 0.0 copy-start.10
  18.3 0.0 copy-done.8
  18.3 0.8 fusion.21
  19.1 0.2 fusion.4
  19.3 0.5 copy-done.4
  19.8 0.1 copy-done.5
  19.9 0.2 copy-done.10
  20.1 0.6 fusion.12
  20.7 0.3 multiply_convert_fusion.3
  21.1 0.4 fusion.22
  21.5 0.0 copy-start.7
  21.5 1.9 multiply_convert_fusion
  23.4 0.0 copy-done.7
  23.4 0.0 copy-start.2
  23.4 0.8 convolution_multiply_fusion.1
  24.3 0.4 convolution_multiply_fusion
  24.7 0.9 copy-done.2
  25.6 1.5 fusion
  27.1 0.0 copy-done.11
  27.2 0.0 copy-start.1
  27.2 3.3 convolution_bitcast_fusion
  30.4 0.0 copy-done.1
  30.4 1.4 fusion.23
  31.9 0.0 all-reduce.5.cloned.1.call-update
  31.9 0.0 all-reduce.7.cloned.1.call-start
  31.9 95.6 %all-reduce.5.cloned.1.call-done = (f32[512,2048]{0,1:T(8,128)}, f32[512,512]{1,0:T(8,128)}) async-done(((f32[512,2048]{0,1:T(8,128)}, f32[512,512]{1,0:T(8,128)}), (f32[512,2048]{0,1:T(8,128)}, f32[512,512]{1,0:T(8,128)})) %all-reduce.5.cloned.1.call-update) | async-done | bytes 5242896 | tf_op jit(solution)/shard_map/psum | solution.py:16
  127.5 0.0 all-reduce.7.cloned.1.call-update
  127.6 0.0 copy-done.12
  127.6 1.2 reduce-window.18
  128.8 0.2 slice_reduce_fusion
  129.0 0.1 fusion.15
  129.2 2.4 scatter_custom_fusion
  131.6 0.7 all_to_all.9
  132.3 4.7 %all-to-all-start = ((s32[32,1,32]{2,1,0:T(1,128)}), s32[32,1,32]{2,1,0:T(1,128)S(1)}, u32[]{:S(2)}, u32[]{:S(2)}) async-start(s32[32,1,32]{2,1,0:T(1,128)} %all_to_all.9), calls=%async_computation | async-start | bytes 32768 | tf_op jit(solution)/shard_map/all_to_all | solution.py:149
  137.0 3.9 %convolution_add_fusion = f32[512,512]{1,0:T(8,128)} fusion(bf16[512,2048]{0,1:T(8,128)(2,1)} %copy-done.1, bf16[512,2048]{1,0:T(8,128)(2,1)S(1)} %copy-done, bf16[512,512]{1,0:T(8,128)(2,1)S(1)} %copy-done.5), kind=kOutput, calls=%fused_computation.16 | convolution fusion | flops 1074266112 | bytes 5767168 | tf_op jit(solution)/shard_map/dot_general | solution.py:141
  140.8 4.3 %scatter_custom_fusion.1 = f32[1024,512]{1,0:T(8,128)} fusion(s32[512]{0:T(512)S(1)} %compare_select_fusion.1, f32[512,512]{1,0:T(8,128)} %convolution_add_fusion, f32[]{:T(128)} %constant.80.clone.1), kind=kCustom, calls=%fused_computation.28 | custom fusion | bytes 2097664 | tf_op jit(solution)/shard_map/scatter | solution.py:99
  145.2 0.0 all-to-all-done
  145.2 5.9 %all-to-all-start.1 = ((f32[32,32,512]{2,1,0:T(8,128)}), f32[32,32,512]{2,1,0:T(8,128)}, u32[]{:S(2)}, u32[]{:S(2)}) async-start(f32[32,32,512]{2,1,0:T(8,128)} %bitcast.81), calls=%async_computation.1 | async-start | bytes 4194304 | tf_op jit(solution)/shard_map/all_to_all | solution.py:148
  151.1 0.5 broadcast.203
  151.6 0.7 reduce.8
  152.3 0.1 reshape.200
  152.4 104.2 %all-to-all-done.1 = f32[32,32,512]{2,1,0:T(8,128)} async-done(((f32[32,32,512]{2,1,0:T(8,128)}), f32[32,32,512]{2,1,0:T(8,128)}, u32[]{:S(2)}, u32[]{:S(2)}) %all-to-all-start.1) | async-done | bytes 2097184 | tf_op jit(solution)/shard_map/all_to_all | solution.py:148
  256.6 8.7 %scatter_custom_fusion.2 = f32[1024,512]{1,0:T(8,128)} fusion(s32[1024]{0:T(1024)S(1)} %bitcast.94, f32[1024,512]{1,0:T(8,128)} %bitcast.18, f32[]{:T(128)} %constant.80.clone.1), kind=kCustom, calls=%fused_computation.26 | custom fusion | flops 524288 | bytes 2097664 | tf_op jit(solution)/shard_map/scatter-add | solution.py:154
  265.3 98.9 %all-reduce.7.cloned.1.call-done = (f32[512,2048]{0,1:T(8,128)}, f32[512,512]{1,0:T(8,128)}) async-done(((f32[512,2048]{0,1:T(8,128)}, f32[512,512]{1,0:T(8,128)}), (f32[512,2048]{0,1:T(8,128)}, f32[512,512]{1,0:T(8,128)})) %all-reduce.7.cloned.1.call-update) | async-done | bytes 5242896 | tf_op jit(solution)/shard_map/psum | solution.py:17
  364.2 4.7 %broadcast_multiply_fusion = f32[512,2048]{0,1:T(8,128)} fusion(f32[512,2048]{0,1:T(8,128)} %get-tuple-element.40), kind=kLoop, calls=%fused_computation.11 | loop fusion | flops 1048576 | bytes 8388608 | tf_op jit(solution)/shard_map/mul | solution.py:157
  368.9 5.4 %copy.34 = f32[512,2048]{1,0:T(8,128)} copy(f32[512,2048]{0,1:T(8,128)} %broadcast_multiply_fusion) | data formatting | bytes 8388608
  374.3 0.0 copy-done.9
  374.3 1.1 broadcast_multiply_fusion.1
  (14 shorter events, 0.1 us)
Async XLA Ops:
  7.2 1.6 copy-start
  7.2 8.7 %copy-start.13 = (s32[1,8]{1,0:T(1,128)S(1)}, s32[1,8]{1,0:T(1,128)}, u32[]{:S(2)}) copy-start(s32[1,8]{1,0:T(1,128)} %param.10) | copy-start | bytes 100
  7.2 120.3 %all-reduce.5.cloned.1.call-start = ((), (), s32[]{:S(2)}) async-start(), calls=%async_computation.2 | async-start | bytes 10485760 | tf_op jit(solution)/shard_map/psum | solution.py:16
  13.6 1.3 copy-start.3
  15.9 0.8 copy-start.6
  16.7 1.6 copy-start.8
  18.2 1.6 copy-start.4
  18.3 1.7 copy-start.5
  18.3 1.8 copy-start.10
  21.5 1.9 copy-start.7
  23.4 2.2 copy-start.2
  25.6 1.5 copy-start.11
  27.2 3.3 copy-start.1
  31.8 95.7 %copy-start.12 = (s32[512]{0:T(512)S(1)}, s32[512]{0:T(512)}, u32[]{:S(2)}) copy-start(s32[512]{0:T(512)} %param.11) | copy-start | bytes 6148
  31.9 332.4 %all-reduce.7.cloned.1.call-start = ((), (), s32[]{:S(2)}) async-start(), calls=%async_computation.3 | async-start | bytes 10485760 | tf_op jit(solution)/shard_map/psum | solution.py:17
  132.3 12.9 %all-to-all-start = ((s32[32,1,32]{2,1,0:T(1,128)}), s32[32,1,32]{2,1,0:T(1,128)S(1)}, u32[]{:S(2)}, u32[]{:S(2)}) async-start(s32[32,1,32]{2,1,0:T(1,128)} %all_to_all.9), calls=%async_computation | async-start | bytes 32768 | tf_op jit(solution)/shard_map/all_to_all | solution.py:149
  145.2 111.5 %all-to-all-start.1 = ((f32[32,32,512]{2,1,0:T(8,128)}), f32[32,32,512]{2,1,0:T(8,128)}, u32[]{:S(2)}, u32[]{:S(2)}) async-start(f32[32,32,512]{2,1,0:T(8,128)} %bitcast.81), calls=%async_computation.1 | async-start | bytes 4194304 | tf_op jit(solution)/shard_map/all_to_all | solution.py:148
  368.9 5.4 %copy-start.9 = (f32[512,512]{1,0:T(8,128)S(1)}, f32[512,512]{1,0:T(8,128)}, u32[]{:S(2)}) copy-start(f32[512,512]{1,0:T(8,128)} %get-tuple-element.41) | copy-start | bytes 3145732
Sparse Core Ops, SparseCore 0:
  32.0 95.4 all-reduce.4
  130.1 234.0 all-reduce.6
